TPU v7x, 256 devices: a whole 4x4x8 slice. The times are simulated.
256 devices in a mesh: dom: 8 (over y, x_lo), sub: 32 (over z, x_hi, core).
Axes of the slice: x: 4 (x_hi: 2, x_lo: 2; x = x_hi * 2 + x_lo), y: 4, z: 8, core: 2. Of those that a mesh axis runs over, the one named last changes fastest.
Arguments:
- fine_residual: float32 [3, 1048576], P(None, ('dom', 'sub')), may hold values from -6 to 6
- bonds: bfloat16 [32, 3, 3, 1048576], P(None, None, None, ('dom', 'sub')), may hold values from -0.3125 to 0.3125
- bond_col: int32 [32, 1048576], P(None, ('dom', 'sub')), may hold values from 0 to 5119, as said below
- ghost_points: int32 [256, 2, 512], P(('dom', 'sub')), may hold values from -1 to 4095, as said below
- fine_dinv: float32 [3, 3, 1048576], P(None, None, ('dom', 'sub')), may hold values from -0.2 to 1.6
- aggregate: int32 [1048576], P(('dom', 'sub')), may hold values from 0 to 131071, as said below
- coarse_dinv: float32 [3, 3, 131072], P(None, None, 'sub'), may hold values from -0.071 to 0.566
- coarse_couple: float32 [4, 131072], P(None, 'sub'), may hold values from 0.08 to 0.24
Outputs:
- preconditioned: float32 [3, 1048576], P(None, ('dom', 'sub'))
Inputs may be any that keep to these rules, and one draw needn't show every extreme that they name: ghost_points[r, 0, :] lists distinct local points of the previous run of r, ghost_points[r, 1, :] of the next run; each list holds 128 to 512 entries, followed by -1; in every draw some run has both lists full. bond_col[0, i] is i's own local index; a column below 4096 is a local point of the run, 4096 + s names slot s from the previous run and 4608 + s slot s from the next run; only slots that hold a point are named. A point of a run with sub-partition index s lies in an aggregate s * 4096 to (s + 1) * 4096 - 1.
All inputs are finite; a program needn't handle non-finite values.
Results may differ from a plain program's by a relative error of at most 0.0014.
Values may be sent and summed in bfloat16 or wider, within the bound.
No kernel may reach another device: no remote copies, remote signals or barrier semaphores. Data moves between devices by JAX's collectives and lax.ppermute only.
A program may use at most 64 MiB of HBM per device.

v0:
```python
import math
import jax
import jax.numpy as jnp
from jax import lax
from jax.sharding import PartitionSpec as P

SWEEPS = 3
JAC = 6
LOW_EIG = 0.3
HIGH_EIG = 2.2


def with_halo(x, sides, width, wrap):
    for axis, dim in sides:
        peers, length = (lax.axis_size(axis), x.shape[dim])
        up = [(i, (i + 1) % peers) for i in range(peers if wrap else peers - 1)]
        down = [(j, i) for i, j in up]
        last = lax.slice_in_dim(x, length - width, length, axis=dim)
        initial = lax.slice_in_dim(x, 0, width, axis=dim)
        before = lax.ppermute(last, axis, up)
        after = lax.ppermute(initial, axis, down)
        x = jnp.concatenate([before, x, after], axis=dim)
    return x


def passed_along(value, axis, steps):
    count = lax.axis_size(axis)
    pairs = [(source, (source + steps) % count) for source in range(count)]
    return lax.ppermute(value, axis, pairs)


def shortened(x):

    def short(part):
        return part.astype(jnp.bfloat16) if part.dtype == jnp.float32 else part

    return jax.tree.map(short, x)


def point_solve(matrix, vector):
    return jnp.sum(matrix * vector[None, :, :], axis=1)


def lookup(table, indices, precision):
    rows = table.shape[0]
    width = table.shape[1]
    groups = -(-width // 128)
    padded = table.reshape(rows * groups, 128)
    flat = indices.reshape(-1)
    total = flat.shape[0]
    block = math.gcd(total, 8192)
    lanes = jnp.arange(128, dtype=jnp.int32)
    group_ids = jnp.arange(groups, dtype=jnp.int32)

    def lookup_one_block(piece):
        onehot = (piece[None, :] % 128 == lanes[:, None]).astype(table.dtype)
        spread = jnp.dot(
            padded, onehot, preferred_element_type=jnp.float32, precision=precision
        ).reshape(rows, groups, block)
        chosen = piece[None, :] // 128 == group_ids[:, None]
        return jnp.sum(jnp.where(chosen[None, :, :], spread, 0.0), axis=1)

    result = lax.map(lookup_one_block, flat.reshape(total // block, block))
    return result.transpose(1, 0, 2).reshape((rows,) + indices.shape)


def accumulate(values, targets, count):
    points = values.shape[1]
    groups = -(-count // 128)
    block = math.gcd(points, 2048)
    lanes = jnp.arange(128, dtype=jnp.int32)
    group_ids = jnp.arange(groups, dtype=jnp.int32)
    value_blocks = values.reshape(3, points // block, block).transpose(1, 0, 2)
    target_blocks = targets.reshape(points // block, block)

    def accumulate_one_block(total, pieces):
        piece_values, piece_targets = pieces
        onehot = (piece_targets[:, None] % 128 == lanes[None, :]).astype(jnp.float32)
        chosen = piece_targets[None, :] // 128 == group_ids[:, None]
        spread = jnp.where(chosen[None, :, :], piece_values[:, None, :], 0.0).reshape(
            3 * groups, block
        )
        return (
            total
            + jnp.dot(
                spread, onehot, preferred_element_type=jnp.float32, precision=lax.Precision.HIGHEST
            ),
            None,
        )

    start = jnp.zeros((3 * groups, 128), jnp.float32)
    total, unused = lax.scan(accumulate_one_block, start, (value_blocks, target_blocks))
    return total.reshape(3, groups * 128)


def body(
    fine_residual, bonds, bond_col, ghost_points, fine_dinv, aggregate, coarse_dinv, coarse_couple
):
    wanted_lists = with_halo(ghost_points, (("sub", 0),), 1, True)
    for_next = wanted_lists[2, 0]
    for_prev = wanted_lists[0, 1]
    center_eig = (HIGH_EIG + LOW_EIG) / 2.0
    half_range = (HIGH_EIG - LOW_EIG) / 2.0
    factor = half_range / center_eig
    update = point_solve(fine_dinv, fine_residual) / center_eig
    smoothed = update
    for iteration in range(SWEEPS):
        packed = smoothed.astype(jnp.bfloat16)

        def select_points(wanted):
            picked = lookup(packed, jnp.maximum(wanted, 0), None)
            return jnp.where(wanted[None, :] >= 0, picked, 0.0).astype(jnp.bfloat16)

        from_prev = passed_along(select_points(for_next), "sub", 1)
        from_next = passed_along(select_points(for_prev), "sub", -1)
        gathered = lookup(
            jnp.concatenate([packed, from_prev, from_next], axis=1), bond_col, None
        ).astype(jnp.bfloat16)
        remainder = (
            fine_residual
            - smoothed
            - jnp.einsum("kcep,ekp->cp", bonds, gathered, preferred_element_type=jnp.float32)
        )
        factor_new = 1.0 / (2.0 * center_eig / half_range - factor)
        update = factor_new * factor * update + 2.0 * factor_new / half_range * point_solve(
            fine_dinv, remainder
        )
        smoothed = smoothed + update
        factor = factor_new
    per_group = coarse_dinv.shape[2]
    local_agg = aggregate - lax.axis_index("sub") * per_group
    rhs_part = accumulate(fine_residual, local_agg, per_group)
    coarse_rhs = lax.psum(rhs_part, "dom")
    coarse_base = point_solve(coarse_dinv, coarse_rhs)
    coarse = coarse_base
    for iteration in range(JAC - 1):
        layers = with_halo(shortened(coarse[None]), (("sub", 0),), 1, False)
        border = jnp.zeros((3, 1), jnp.float32)
        before = jnp.concatenate([border, coarse[:, :-1]], axis=1)
        after = jnp.concatenate([coarse[:, 1:], border], axis=1)
        below, above, before, after = (layers[0], layers[2], before, after)
        coarse = coarse_base + (
            coarse_couple[0] * below
            + coarse_couple[1] * above
            + coarse_couple[2] * before
            + coarse_couple[3] * after
        )
    return smoothed + lookup(coarse, local_agg, lax.Precision.HIGHEST)


def solution(mesh):
    placed = (
        P(None, ("dom", "sub")),
        P(None, None, None, ("dom", "sub")),
        P(None, ("dom", "sub")),
        P(("dom", "sub"), None, None),
        P(None, None, ("dom", "sub")),
        P(("dom", "sub")),
        P(None, None, "sub"),
        P(None, "sub"),
    )
    return jax.shard_map(
        body, mesh=mesh, in_specs=placed, out_specs=P(None, ("dom", "sub")), check_vma=False
    )
```

profile of v0, /device:TPU:101, one launch (start us, length us, event | category | flops | bytes accessed | tf_op | source)
XLA Modules:
  0.0 297.3 jit_solution(10661571524658893954)
XLA Ops:
  0.7 4.7 %collective-permute-start.2 = (s32[1,2,512]{2,1,0:T(2,128)}, s32[1,2,512]{2,1,0:T(2,128)S(1)}, u32[]{:S(2)}, u32[]{:S(2)}) collective-permute-start(s32[1,2,512]{2,1,0:T(2,128)} %param.19), channel_id=1, source_target_pairs={{0,1},{1,2},{2,3},{3,4},{4,5},{5,6},{6,7},{7,8},{8,9},{9,10},{10,1... | collective-permute-start | bytes 12296 | tf_op jit(solution)/shard_map/ppermute | solution.py:20
  6.7 3.5 %while.39 = (s32[]{:T(128)}, f32[96,128]{1,0:T(8,128)S(1)}, s32[2,2048]{1,0:T(2,128)S(1)}, f32[2,3,2048]{2,1,0:T(4,128)}, s32[]{:T(128)}, /*index=5*/s32[]{:T(128)}) while((s32[]{:T(128)}, f32[96,128]{1,0:T(8,128)S(1)}, s32[2,2048]{1,0:T(2,128)S(1)}, f32[2,3,2048]{2,1,0:T(4,128)}, s32[]{:T(128)}, /*index=5*/s32[]{:T(128)}) %tuple.160), condition=%wide.region_20.21_spmd.clone, body=%wide.region_19.20_spmd.clone.sunk | while | flops 302592000 | bytes 1933399 | solution.py:92
  10.2 27.8 %psum.7 = f32[3,4096]{1,0:T(4,128)S(1)} all-reduce(f32[3,4096]{1,0:T(4,128)S(1)} %reshape.539), channel_id=1, replica_groups=mesh['dom'=8,'sub'=32] {'dom'}, use_global_device_ids=true, to_apply=%region_21.22 | all-reduce | flops 12288 | bytes 98304 | tf_op jit(solution)/shard_map/psum | solution.py:133
  38.7 8.5 %collective-permute-start.8 = (bf16[1,3,4096]{2,1,0:T(4,128)(2,1)}, bf16[1,3,4096]{2,1,0:T(4,128)(2,1)}, u32[]{:S(2)}, u32[]{:S(2)}) collective-permute-start(bf16[1,3,4096]{2,1,0:T(4,128)(2,1)} %convert_bitcast_fusion.7), channel_id=1, source_target_pairs={{0,1},{1,2},{2,3},{3,4},{4,5},{5,6},{6,7},{7,8},{8,9},{9,10},{10,1... | collective-permute-start | bytes 73736 | tf_op jit(solution)/shard_map/ppermute | solution.py:20
  47.2 1.9 collective-permute-start.9
  52.0 5.4 %collective-permute-start.1 = (bf16[3,512]{1,0:T(4,128)(2,1)S(1)}, bf16[3,512]{1,0:T(4,128)(2,1)S(1)}, u32[]{:S(2)}, u32[]{:S(2)}) collective-permute-start(bf16[3,512]{1,0:T(4,128)(2,1)S(1)} %select_convert_fusion.5), channel_id=1, source_target_pairs={{0,1},{1,2},{2,3},{3,4},{4,5},{5,6},{6,7},{7,8},{8,9},{9,10},{10,1... | collective-permute-start | bytes 9224 | tf_op jit(solution)/shard_map/ppermute | solution.py:29
  59.1 5.6 %collective-permute-done.3 = bf16[3,512]{1,0:T(4,128)(2,1)S(1)} collective-permute-done((bf16[3,512]{1,0:T(4,128)(2,1)S(1)}, bf16[3,512]{1,0:T(4,128)(2,1)S(1)}, u32[]{:S(2)}, u32[]{:S(2)}) %collective-permute-start.3) | collective-permute-done | bytes 3104 | tf_op jit(solution)/shard_map/ppermute | solution.py:29
  65.2 43.8 %while.36 = (s32[]{:T(128)}, bf16[16,3,8192]{2,1,0:T(4,128)(2,1)S(1)}, s32[16,8192]{1,0:T(8,128)}, bf16[120,128]{1,0:T(8,128)(2,1)S(1)}, s32[]{:T(128)}) while((s32[]{:T(128)}, bf16[16,3,8192]{2,1,0:T(4,128)(2,1)S(1)}, s32[16,8192]{1,0:T(8,128)}, bf16[120,128]{1,0:T(8,128)(2,1)S(1)}, s32[]{:T(128)}) %tuple.151), condition=%wide.region_5.6_spmd.clone, body=%wide.region_3.5_spmd.clone.sunk | while | flops 255139840 | bytes 8960069 | solution.py:63
  115.6 5.5 %collective-permute-done.5 = bf16[3,512]{1,0:T(4,128)(2,1)S(1)} collective-permute-done((bf16[3,512]{1,0:T(4,128)(2,1)S(1)}, bf16[3,512]{1,0:T(4,128)(2,1)S(1)}, u32[]{:S(2)}, u32[]{:S(2)}) %collective-permute-start.5) | collective-permute-done | bytes 3104 | tf_op jit(solution)/shard_map/ppermute | solution.py:29
  122.2 55.9 %while.37 = (s32[]{:T(128)}, bf16[16,3,8192]{2,1,0:T(4,128)(2,1)S(1)}, s32[16,8192]{1,0:T(8,128)}, bf16[120,128]{1,0:T(8,128)(2,1)}, s32[]{:T(128)}) while((s32[]{:T(128)}, bf16[16,3,8192]{2,1,0:T(4,128)(2,1)S(1)}, s32[16,8192]{1,0:T(8,128)}, bf16[120,128]{1,0:T(8,128)(2,1)}, s32[]{:T(128)}) %tuple.154), condition=%wide.region_11.12_spmd.clone, body=%wide.region_9.11_spmd.clone.sunk | while | flops 255139840 | bytes 8960069 | solution.py:63
  184.5 5.6 %collective-permute-done.7 = bf16[3,512]{1,0:T(4,128)(2,1)S(1)} collective-permute-done((bf16[3,512]{1,0:T(4,128)(2,1)S(1)}, bf16[3,512]{1,0:T(4,128)(2,1)S(1)}, u32[]{:S(2)}, u32[]{:S(2)}) %collective-permute-start.7) | collective-permute-done | bytes 3104 | tf_op jit(solution)/shard_map/ppermute | solution.py:29
  191.2 55.8 %while.38 = (s32[]{:T(128)}, bf16[16,3,8192]{2,1,0:T(4,128)(2,1)S(1)}, s32[16,8192]{1,0:T(8,128)}, bf16[120,128]{1,0:T(8,128)(2,1)}, s32[]{:T(128)}) while((s32[]{:T(128)}, bf16[16,3,8192]{2,1,0:T(4,128)(2,1)S(1)}, s32[16,8192]{1,0:T(8,128)}, bf16[120,128]{1,0:T(8,128)(2,1)}, s32[]{:T(128)}) %tuple.157), condition=%wide.region_17.18_spmd.clone, body=%wide.region_15.17_spmd.clone.sunk | while | flops 255139840 | bytes 8960069 | solution.py:63
  251.9 2.0 collective-permute-start.10
  253.8 2.4 collective-permute-start.11
  256.3 6.4 %collective-permute-done.11 = bf16[1,3,4096]{2,1,0:T(4,128)(2,1)S(1)} collective-permute-done((bf16[1,3,4096]{2,1,0:T(4,128)(2,1)S(1)}, bf16[1,3,4096]{2,1,0:T(4,128)(2,1)S(1)}, u32[]{:S(2)}, u32[]{:S(2)}) %collective-permute-start.11) | collective-permute-done | bytes 24608 | tf_op jit(solution)/shard_map/ppermute | solution.py:21
  262.8 1.9 collective-permute-start.12
  264.7 2.4 collective-permute-start.13
  267.3 6.3 %collective-permute-done.13 = bf16[1,3,4096]{2,1,0:T(4,128)(2,1)S(1)} collective-permute-done((bf16[1,3,4096]{2,1,0:T(4,128)(2,1)S(1)}, bf16[1,3,4096]{2,1,0:T(4,128)(2,1)S(1)}, u32[]{:S(2)}, u32[]{:S(2)}) %collective-permute-start.13) | collective-permute-done | bytes 24608 | tf_op jit(solution)/shard_map/ppermute | solution.py:21
  273.7 1.9 collective-permute-start.14
  275.6 2.4 collective-permute-start.15
  278.1 6.3 %collective-permute-done.15 = bf16[1,3,4096]{2,1,0:T(4,128)(2,1)S(1)} collective-permute-done((bf16[1,3,4096]{2,1,0:T(4,128)(2,1)S(1)}, bf16[1,3,4096]{2,1,0:T(4,128)(2,1)S(1)}, u32[]{:S(2)}, u32[]{:S(2)}) %collective-permute-start.15) | collective-permute-done | bytes 24608 | tf_op jit(solution)/shard_map/ppermute | solution.py:21
  284.6 1.9 collective-permute-start.16
  286.5 2.4 collective-permute-start.17
  289.0 6.3 %collective-permute-done.17 = bf16[1,3,4096]{2,1,0:T(4,128)(2,1)S(1)} collective-permute-done((bf16[1,3,4096]{2,1,0:T(4,128)(2,1)S(1)}, bf16[1,3,4096]{2,1,0:T(4,128)(2,1)S(1)}, u32[]{:S(2)}, u32[]{:S(2)}) %collective-permute-start.17) | collective-permute-done | bytes 24608 | tf_op jit(solution)/shard_map/ppermute | solution.py:21
  (477 shorter events, 186.2 us)
Async XLA Ops:
  0.0 51.6 %collective-permute-start = (s32[1,2,512]{2,1,0:T(2,128)}, s32[1,2,512]{2,1,0:T(2,128)S(1)}, u32[]{:S(2)}, u32[]{:S(2)}) collective-permute-start(s32[1,2,512]{2,1,0:T(2,128)} %param.19), channel_id=1, source_target_pairs={{1,0},{2,1},{3,2},{4,3},{5,4},{6,5},{7,6},{8,7},{9,8},{10,9},{11,1... | collective-permute-start | bytes 12296 | tf_op jit(solution)/shard_map/ppermute | solution.py:21
  0.7 56.7 %collective-permute-start.2 = (s32[1,2,512]{2,1,0:T(2,128)}, s32[1,2,512]{2,1,0:T(2,128)S(1)}, u32[]{:S(2)}, u32[]{:S(2)}) collective-permute-start(s32[1,2,512]{2,1,0:T(2,128)} %param.19), channel_id=1, source_target_pairs={{0,1},{1,2},{2,3},{3,4},{4,5},{5,6},{6,7},{7,8},{8,9},{9,10},{10,1... | collective-permute-start | bytes 12296 | tf_op jit(solution)/shard_map/ppermute | solution.py:20
  6.1 52.0 %copy-start.17 = (s32[32,4096]{1,0:T(8,128)S(1)}, s32[32,4096]{1,0:T(8,128)}, u32[]{:S(2)}) copy-start(s32[32,4096]{1,0:T(8,128)} %param.18) | copy-start | bytes 1572868
  38.7 212.2 %collective-permute-start.8 = (bf16[1,3,4096]{2,1,0:T(4,128)(2,1)}, bf16[1,3,4096]{2,1,0:T(4,128)(2,1)}, u32[]{:S(2)}, u32[]{:S(2)}) collective-permute-start(bf16[1,3,4096]{2,1,0:T(4,128)(2,1)} %convert_bitcast_fusion.7), channel_id=1, source_target_pairs={{0,1},{1,2},{2,3},{3,4},{4,5},{5,6},{6,7},{7,8},{8,9},{9,10},{10,1... | collective-permute-start | bytes 73736 | tf_op jit(solution)/shard_map/ppermute | solution.py:20
  47.2 203.7 %collective-permute-start.9 = (bf16[1,3,4096]{2,1,0:T(4,128)(2,1)}, bf16[1,3,4096]{2,1,0:T(4,128)(2,1)}, u32[]{:S(2)}, u32[]{:S(2)}) collective-permute-start(bf16[1,3,4096]{2,1,0:T(4,128)(2,1)} %convert_bitcast_fusion.7), channel_id=1, source_target_pairs={{1,0},{2,1},{3,2},{4,3},{5,4},{6,5},{7,6},{8,7},{9,8},{10,9},{11,1... | collective-permute-start | bytes 73736 | tf_op jit(solution)/shard_map/ppermute | solution.py:21
  51.7 61.9 %copy-start.25 = (pred[32,512]{1,0:T(8,128)(4,1)}, pred[32,512]{1,0:T(8,128)(4,1)S(1)}, u32[]{:S(2)}) copy-start(pred[32,512]{1,0:T(8,128)(4,1)S(1)} %iota_compare_fusion.17) | copy-start | bytes 49156
  52.0 7.1 %collective-permute-start.1 = (bf16[3,512]{1,0:T(4,128)(2,1)S(1)}, bf16[3,512]{1,0:T(4,128)(2,1)S(1)}, u32[]{:S(2)}, u32[]{:S(2)}) collective-permute-start(bf16[3,512]{1,0:T(4,128)(2,1)S(1)} %select_convert_fusion.5), channel_id=1, source_target_pairs={{0,1},{1,2},{2,3},{3,4},{4,5},{5,6},{6,7},{7,8},{8,9},{9,10},{10,1... | collective-permute-start | bytes 9224 | tf_op jit(solution)/shard_map/ppermute | solution.py:29
  58.1 6.6 %collective-permute-start.3 = (bf16[3,512]{1,0:T(4,128)(2,1)S(1)}, bf16[3,512]{1,0:T(4,128)(2,1)S(1)}, u32[]{:S(2)}, u32[]{:S(2)}) collective-permute-start(bf16[3,512]{1,0:T(4,128)(2,1)S(1)} %select_convert_fusion.4), channel_id=1, source_target_pairs={{0,31},{1,0},{2,1},{3,2},{4,3},{5,4},{6,5},{7,6},{8,7},{9,8},{10,9... | collective-permute-start | bytes 9224 | tf_op jit(solution)/shard_map/ppermute | solution.py:29
  114.1 1.5 collective-permute-start.4
  114.2 6.9 %collective-permute-start.5 = (bf16[3,512]{1,0:T(4,128)(2,1)S(1)}, bf16[3,512]{1,0:T(4,128)(2,1)S(1)}, u32[]{:S(2)}, u32[]{:S(2)}) collective-permute-start(bf16[3,512]{1,0:T(4,128)(2,1)S(1)} %select_convert_fusion.2), channel_id=1, source_target_pairs={{0,31},{1,0},{2,1},{3,2},{4,3},{5,4},{6,5},{7,6},{8,7},{9,8},{10,9... | collective-permute-start | bytes 9224 | tf_op jit(solution)/shard_map/ppermute | solution.py:29
  183.2 1.3 collective-permute-start.6
  183.4 6.7 %collective-permute-start.7 = (bf16[3,512]{1,0:T(4,128)(2,1)S(1)}, bf16[3,512]{1,0:T(4,128)(2,1)S(1)}, u32[]{:S(2)}, u32[]{:S(2)}) collective-permute-start(bf16[3,512]{1,0:T(4,128)(2,1)S(1)} %select_convert_fusion), channel_id=1, source_target_pairs={{0,31},{1,0},{2,1},{3,2},{4,3},{5,4},{6,5},{7,6},{8,7},{9,8},{10,9... | collective-permute-start | bytes 9224 | tf_op jit(solution)/shard_map/ppermute | solution.py:29
  250.1 45.4 %copy-start.23 = (pred[32,4096]{1,0:T(8,128)(4,1)S(1)}, pred[32,4096]{1,0:T(8,128)(4,1)}, u32[]{:S(2)}) copy-start(pred[32,4096]{1,0:T(8,128)(4,1)} %iota_compare_fusion.13) | copy-start | bytes 393220
  250.1 45.4 %copy-start.30 = (s32[4096]{0:T(1024)S(1)}, s32[4096]{0:T(1024)}, u32[]{:S(2)}) copy-start(s32[4096]{0:T(1024)} %add_select_fusion.1) | copy-start | bytes 49156
  250.1 46.5 %copy-start.10 = (f32[3,4096]{1,0:T(4,128)S(1)}, f32[3,4096]{1,0:T(4,128)}, u32[]{:S(2)}) copy-start(f32[3,4096]{1,0:T(4,128)} %copy-done.8) | copy-start | bytes 147460
  250.1 46.5 %copy-start.12 = (f32[3,4096]{1,0:T(4,128)S(1)}, f32[3,4096]{1,0:T(4,128)}, u32[]{:S(2)}) copy-start(f32[3,4096]{1,0:T(4,128)} %copy-done.11) | copy-start | bytes 147460
  251.9 4.4 %collective-permute-start.10 = (bf16[1,3,4096]{2,1,0:T(4,128)(2,1)S(1)}, bf16[1,3,4096]{2,1,0:T(4,128)(2,1)S(1)}, u32[]{:S(2)}, u32[]{:S(2)}) collective-permute-start(bf16[1,3,4096]{2,1,0:T(4,128)(2,1)S(1)} %get-tuple-element.559), channel_id=1, source_target_pairs={{0,1},{1,2},{2,3},{3,4},{4,5},{5,6},{6,7},{7,8},{8,9},{9,10},{10,1... | collective-permute-start | bytes 73736 | tf_op jit(solution)/shard_map/ppermute | solution.py:20
  253.8 8.8 %collective-permute-start.11 = (bf16[1,3,4096]{2,1,0:T(4,128)(2,1)S(1)}, bf16[1,3,4096]{2,1,0:T(4,128)(2,1)S(1)}, u32[]{:S(2)}, u32[]{:S(2)}) collective-permute-start(bf16[1,3,4096]{2,1,0:T(4,128)(2,1)S(1)} %get-tuple-element.559), channel_id=1, source_target_pairs={{1,0},{2,1},{3,2},{4,3},{5,4},{6,5},{7,6},{8,7},{9,8},{10,9},{11,1... | collective-permute-start | bytes 73736 | tf_op jit(solution)/shard_map/ppermute | solution.py:21
  262.8 4.4 %collective-permute-start.12 = (bf16[1,3,4096]{2,1,0:T(4,128)(2,1)S(1)}, bf16[1,3,4096]{2,1,0:T(4,128)(2,1)S(1)}, u32[]{:S(2)}, u32[]{:S(2)}) collective-permute-start(bf16[1,3,4096]{2,1,0:T(4,128)(2,1)S(1)} %get-tuple-element.557), channel_id=1, source_target_pairs={{0,1},{1,2},{2,3},{3,4},{4,5},{5,6},{6,7},{7,8},{8,9},{9,10},{10,1... | collective-permute-start | bytes 73736 | tf_op jit(solution)/shard_map/ppermute | solution.py:20
  264.7 8.8 %collective-permute-start.13 = (bf16[1,3,4096]{2,1,0:T(4,128)(2,1)S(1)}, bf16[1,3,4096]{2,1,0:T(4,128)(2,1)S(1)}, u32[]{:S(2)}, u32[]{:S(2)}) collective-permute-start(bf16[1,3,4096]{2,1,0:T(4,128)(2,1)S(1)} %get-tuple-element.557), channel_id=1, source_target_pairs={{1,0},{2,1},{3,2},{4,3},{5,4},{6,5},{7,6},{8,7},{9,8},{10,9},{11,1... | collective-permute-start | bytes 73736 | tf_op jit(solution)/shard_map/ppermute | solution.py:21
  273.7 4.4 %collective-permute-start.14 = (bf16[1,3,4096]{2,1,0:T(4,128)(2,1)S(1)}, bf16[1,3,4096]{2,1,0:T(4,128)(2,1)S(1)}, u32[]{:S(2)}, u32[]{:S(2)}) collective-permute-start(bf16[1,3,4096]{2,1,0:T(4,128)(2,1)S(1)} %get-tuple-element.555), channel_id=1, source_target_pairs={{0,1},{1,2},{2,3},{3,4},{4,5},{5,6},{6,7},{7,8},{8,9},{9,10},{10,1... | collective-permute-start | bytes 73736 | tf_op jit(solution)/shard_map/ppermute | solution.py:20
  275.6 8.8 %collective-permute-start.15 = (bf16[1,3,4096]{2,1,0:T(4,128)(2,1)S(1)}, bf16[1,3,4096]{2,1,0:T(4,128)(2,1)S(1)}, u32[]{:S(2)}, u32[]{:S(2)}) collective-permute-start(bf16[1,3,4096]{2,1,0:T(4,128)(2,1)S(1)} %get-tuple-element.555), channel_id=1, source_target_pairs={{1,0},{2,1},{3,2},{4,3},{5,4},{6,5},{7,6},{8,7},{9,8},{10,9},{11,1... | collective-permute-start | bytes 73736 | tf_op jit(solution)/shard_map/ppermute | solution.py:21
  284.6 4.4 %collective-permute-start.16 = (bf16[1,3,4096]{2,1,0:T(4,128)(2,1)S(1)}, bf16[1,3,4096]{2,1,0:T(4,128)(2,1)S(1)}, u32[]{:S(2)}, u32[]{:S(2)}) collective-permute-start(bf16[1,3,4096]{2,1,0:T(4,128)(2,1)S(1)} %get-tuple-element.553), channel_id=1, source_target_pairs={{0,1},{1,2},{2,3},{3,4},{4,5},{5,6},{6,7},{7,8},{8,9},{9,10},{10,1... | collective-permute-start | bytes 73736 | tf_op jit(solution)/shard_map/ppermute | solution.py:20
  286.5 8.8 %collective-permute-start.17 = (bf16[1,3,4096]{2,1,0:T(4,128)(2,1)S(1)}, bf16[1,3,4096]{2,1,0:T(4,128)(2,1)S(1)}, u32[]{:S(2)}, u32[]{:S(2)}) collective-permute-start(bf16[1,3,4096]{2,1,0:T(4,128)(2,1)S(1)} %get-tuple-element.553), channel_id=1, source_target_pairs={{1,0},{2,1},{3,2},{4,3},{5,4},{6,5},{7,6},{8,7},{9,8},{10,9},{11,1... | collective-permute-start | bytes 73736 | tf_op jit(solution)/shard_map/ppermute | solution.py:21
  (37 other events, 156.3 us)
where the time goes:
time: 302 us; the launch traced here: 297 us
  other arithmetic  99.5 us (33%)
  matrix products  65.2 us (22%)
  waiting for transfers between devices  42.1 us (14%)
  starting transfers between devices  40 us (13%)
  blocking collectives  27.8 us (9%)
  local copies, waits for them, and re-layouts  19.2 us (6%)
    dot_general x55, matrix products, lookup_one_block(): jnp.dot(padded, onehot, preferred_element_type=jnp.float32, precision=pre...  63.7 us
    select_n x51, other arithmetic, lookup_one_block(): chosen = piece[None, :] // 128 == group_ids[:, None]  54.6 us
    psum x1, blocking collectives, body(): coarse_rhs = lax.psum(rhs_part, 'dom')  27.8 us
    ppermute x6, waiting for transfers between devices, with_halo(): after = lax.ppermute(initial, axis, down)  25.3 us
    reduce_sum x48, other arithmetic, lookup_one_block(): return jnp.sum(jnp.where(chosen[None, :, :], spread, 0.0), axis=1)  25.3 us
    ppermute x6, starting transfers between devices, with_halo(): before = lax.ppermute(last, axis, up)  20.9 us
    ppermute x6, waiting for transfers between devices, passed_along(): return lax.ppermute(value, axis, pairs)  16.7 us
    ppermute x6, starting transfers between devices, with_halo(): after = lax.ppermute(initial, axis, down)  12.2 us
  transfers between devices with their start and end apart: 18, of which 7 were waited for; matrix products, arithmetic and copies ran while one was open for 60% of the time, Pallas kernels for 0%

commit v1 on v0

--- a/solution.py
+++ b/solution.py
@@ -130,7 +130,7 @@
     per_group = coarse_dinv.shape[2]
     local_agg = aggregate - lax.axis_index("sub") * per_group
     rhs_part = accumulate(fine_residual, local_agg, per_group)
-    coarse_rhs = lax.psum(rhs_part, "dom")
+    coarse_rhs = jnp.sum(lax.all_gather(rhs_part, "dom"), axis=0)
     coarse_base = point_solve(coarse_dinv, coarse_rhs)
     coarse = coarse_base
     for iteration in range(JAC - 1):

time: 302 us -> 298 us (0.987)
    psum x1 -> x0, blocking collectives: 27.8 us -> none  [body(): coarse_rhs = lax.psum(rhs_part, 'dom')]
    all_gather x0 -> x1, blocking collectives: none -> 25.1 us  [body(): coarse_rhs = jnp.sum(lax.all_gather(rhs_part, 'dom'), axis=0)]
  transfers between devices with their start and end apart: 18 -> 18, of which waited for: 7 -> 7; matrix products, arithmetic and copies ran while one was open for 60% -> 61% of each run, Pallas kernels for 0% -> 0%
where the time goes in v1:
time: 298 us; the launch traced here: 293 us
  other arithmetic  99.6 us (33%)
  matrix products  65.1 us (22%)
  waiting for transfers between devices  42.1 us (14%)
  starting transfers between devices  38.6 us (13%)
  blocking collectives  25.1 us (8%)
  local copies, waits for them, and re-layouts  19.2 us (6%)
    dot_general x55, matrix products, lookup_one_block(): jnp.dot(padded, onehot, preferred_element_type=jnp.float32, precision=pre...  63.6 us
    select_n x51, other arithmetic, lookup_one_block(): chosen = piece[None, :] // 128 == group_ids[:, None]  54.6 us
    ppermute x6, waiting for transfers between devices, with_halo(): after = lax.ppermute(initial, axis, down)  25.3 us
    reduce_sum x48, other arithmetic, lookup_one_block(): return jnp.sum(jnp.where(chosen[None, :, :], spread, 0.0), axis=1)  25.3 us
    all_gather x1, blocking collectives, body(): coarse_rhs = jnp.sum(lax.all_gather(rhs_part, 'dom'), axis=0)  25.1 us
    ppermute x6, starting transfers between devices, with_halo(): before = lax.ppermute(last, axis, up)  19.4 us
    ppermute x6, waiting for transfers between devices, passed_along(): return lax.ppermute(value, axis, pairs)  16.7 us
    ppermute x6, starting transfers between devices, with_halo(): after = lax.ppermute(initial, axis, down)  12.2 us
  transfers between devices with their start and end apart: 18, of which 7 were waited for; matrix products, arithmetic and copies ran while one was open for 61% of the time, Pallas kernels for 0%

profile of v1, /device:TPU:101, one launch (start us, length us, event | category | flops | bytes accessed | tf_op | source)
XLA Modules:
  0.0 293.2 jit_solution(13204789894431686923)
XLA Ops:
  0.7 4.7 %collective-permute-start.2 = (s32[1,2,512]{2,1,0:T(2,128)}, s32[1,2,512]{2,1,0:T(2,128)S(1)}, u32[]{:S(2)}, u32[]{:S(2)}) collective-permute-start(s32[1,2,512]{2,1,0:T(2,128)} %param.19), channel_id=1, source_target_pairs={{0,1},{1,2},{2,3},{3,4},{4,5},{5,6},{6,7},{7,8},{8,9},{9,10},{10,1... | collective-permute-start | bytes 12296 | tf_op jit(solution)/shard_map/ppermute | solution.py:20
  6.7 3.5 %while.39 = (s32[]{:T(128)}, f32[96,128]{1,0:T(8,128)S(1)}, s32[2,2048]{1,0:T(2,128)S(1)}, f32[2,3,2048]{2,1,0:T(4,128)}, s32[]{:T(128)}, /*index=5*/s32[]{:T(128)}) while((s32[]{:T(128)}, f32[96,128]{1,0:T(8,128)S(1)}, s32[2,2048]{1,0:T(2,128)S(1)}, f32[2,3,2048]{2,1,0:T(4,128)}, s32[]{:T(128)}, /*index=5*/s32[]{:T(128)}) %tuple.160), condition=%wide.region_20.21_spmd.clone, body=%wide.region_19.20_spmd.clone.sunk | while | flops 302592000 | bytes 1933399 | solution.py:92
  10.2 25.1 %all_gather.3 = f32[8,3,4096]{2,1,0:T(4,128)S(1)} all-gather(f32[1,3,4096]{2,1,0:T(4,128)S(1)} %all_gather_reshape.3), channel_id=1, replica_groups=mesh['dom'=8,'sub'=32] {'dom'}, dimensions={0}, use_global_device_ids=true | all-gather | bytes 442368 | tf_op jit(solution)/shard_map/all_gather | solution.py:133
  36.1 7.1 %collective-permute-start.8 = (bf16[1,3,4096]{2,1,0:T(4,128)(2,1)}, bf16[1,3,4096]{2,1,0:T(4,128)(2,1)}, u32[]{:S(2)}, u32[]{:S(2)}) collective-permute-start(bf16[1,3,4096]{2,1,0:T(4,128)(2,1)} %convert_bitcast_fusion.7), channel_id=1, source_target_pairs={{0,1},{1,2},{2,3},{3,4},{4,5},{5,6},{6,7},{7,8},{8,9},{9,10},{10,1... | collective-permute-start | bytes 73736 | tf_op jit(solution)/shard_map/ppermute | solution.py:20
  43.2 1.9 collective-permute-start.9
  47.9 5.4 %collective-permute-start.1 = (bf16[3,512]{1,0:T(4,128)(2,1)S(1)}, bf16[3,512]{1,0:T(4,128)(2,1)S(1)}, u32[]{:S(2)}, u32[]{:S(2)}) collective-permute-start(bf16[3,512]{1,0:T(4,128)(2,1)S(1)} %select_convert_fusion.5), channel_id=1, source_target_pairs={{0,1},{1,2},{2,3},{3,4},{4,5},{5,6},{6,7},{7,8},{8,9},{9,10},{10,1... | collective-permute-start | bytes 9224 | tf_op jit(solution)/shard_map/ppermute | solution.py:29
  55.1 5.6 %collective-permute-done.3 = bf16[3,512]{1,0:T(4,128)(2,1)S(1)} collective-permute-done((bf16[3,512]{1,0:T(4,128)(2,1)S(1)}, bf16[3,512]{1,0:T(4,128)(2,1)S(1)}, u32[]{:S(2)}, u32[]{:S(2)}) %collective-permute-start.3) | collective-permute-done | bytes 3104 | tf_op jit(solution)/shard_map/ppermute | solution.py:29
  61.2 43.8 %while.36 = (s32[]{:T(128)}, bf16[16,3,8192]{2,1,0:T(4,128)(2,1)S(1)}, s32[16,8192]{1,0:T(8,128)}, bf16[120,128]{1,0:T(8,128)(2,1)S(1)}, s32[]{:T(128)}) while((s32[]{:T(128)}, bf16[16,3,8192]{2,1,0:T(4,128)(2,1)S(1)}, s32[16,8192]{1,0:T(8,128)}, bf16[120,128]{1,0:T(8,128)(2,1)S(1)}, s32[]{:T(128)}) %tuple.151), condition=%wide.region_5.6_spmd.clone, body=%wide.region_3.5_spmd.clone.sunk | while | flops 255139840 | bytes 8960069 | solution.py:63
  111.6 5.5 %collective-permute-done.5 = bf16[3,512]{1,0:T(4,128)(2,1)S(1)} collective-permute-done((bf16[3,512]{1,0:T(4,128)(2,1)S(1)}, bf16[3,512]{1,0:T(4,128)(2,1)S(1)}, u32[]{:S(2)}, u32[]{:S(2)}) %collective-permute-start.5) | collective-permute-done | bytes 3104 | tf_op jit(solution)/shard_map/ppermute | solution.py:29
  118.2 55.8 %while.37 = (s32[]{:T(128)}, bf16[16,3,8192]{2,1,0:T(4,128)(2,1)S(1)}, s32[16,8192]{1,0:T(8,128)}, bf16[120,128]{1,0:T(8,128)(2,1)}, s32[]{:T(128)}) while((s32[]{:T(128)}, bf16[16,3,8192]{2,1,0:T(4,128)(2,1)S(1)}, s32[16,8192]{1,0:T(8,128)}, bf16[120,128]{1,0:T(8,128)(2,1)}, s32[]{:T(128)}) %tuple.154), condition=%wide.region_11.12_spmd.clone, body=%wide.region_9.11_spmd.clone.sunk | while | flops 255139840 | bytes 8960069 | solution.py:63
  180.4 5.6 %collective-permute-done.7 = bf16[3,512]{1,0:T(4,128)(2,1)S(1)} collective-permute-done((bf16[3,512]{1,0:T(4,128)(2,1)S(1)}, bf16[3,512]{1,0:T(4,128)(2,1)S(1)}, u32[]{:S(2)}, u32[]{:S(2)}) %collective-permute-start.7) | collective-permute-done | bytes 3104 | tf_op jit(solution)/shard_map/ppermute | solution.py:29
  187.0 55.8 %while.38 = (s32[]{:T(128)}, bf16[16,3,8192]{2,1,0:T(4,128)(2,1)S(1)}, s32[16,8192]{1,0:T(8,128)}, bf16[120,128]{1,0:T(8,128)(2,1)}, s32[]{:T(128)}) while((s32[]{:T(128)}, bf16[16,3,8192]{2,1,0:T(4,128)(2,1)S(1)}, s32[16,8192]{1,0:T(8,128)}, bf16[120,128]{1,0:T(8,128)(2,1)}, s32[]{:T(128)}) %tuple.157), condition=%wide.region_17.18_spmd.clone, body=%wide.region_15.17_spmd.clone.sunk | while | flops 255139840 | bytes 8960069 | solution.py:63
  247.7 1.9 collective-permute-start.10
  249.7 2.4 collective-permute-start.11
  252.2 6.3 %collective-permute-done.11 = bf16[1,3,4096]{2,1,0:T(4,128)(2,1)S(1)} collective-permute-done((bf16[1,3,4096]{2,1,0:T(4,128)(2,1)S(1)}, bf16[1,3,4096]{2,1,0:T(4,128)(2,1)S(1)}, u32[]{:S(2)}, u32[]{:S(2)}) %collective-permute-start.11) | collective-permute-done | bytes 24608 | tf_op jit(solution)/shard_map/ppermute | solution.py:21
  258.6 1.9 collective-permute-start.12
  260.6 2.4 collective-permute-start.13
  263.1 6.3 %collective-permute-done.13 = bf16[1,3,4096]{2,1,0:T(4,128)(2,1)S(1)} collective-permute-done((bf16[1,3,4096]{2,1,0:T(4,128)(2,1)S(1)}, bf16[1,3,4096]{2,1,0:T(4,128)(2,1)S(1)}, u32[]{:S(2)}, u32[]{:S(2)}) %collective-permute-start.13) | collective-permute-done | bytes 24608 | tf_op jit(solution)/shard_map/ppermute | solution.py:21
  269.5 1.9 collective-permute-start.14
  271.5 2.4 collective-permute-start.15
  274.0 6.3 %collective-permute-done.15 = bf16[1,3,4096]{2,1,0:T(4,128)(2,1)S(1)} collective-permute-done((bf16[1,3,4096]{2,1,0:T(4,128)(2,1)S(1)}, bf16[1,3,4096]{2,1,0:T(4,128)(2,1)S(1)}, u32[]{:S(2)}, u32[]{:S(2)}) %collective-permute-start.15) | collective-permute-done | bytes 24608 | tf_op jit(solution)/shard_map/ppermute | solution.py:21
  280.4 1.9 collective-permute-start.16
  282.4 2.4 collective-permute-start.17
  284.9 6.3 %collective-permute-done.17 = bf16[1,3,4096]{2,1,0:T(4,128)(2,1)S(1)} collective-permute-done((bf16[1,3,4096]{2,1,0:T(4,128)(2,1)S(1)}, bf16[1,3,4096]{2,1,0:T(4,128)(2,1)S(1)}, u32[]{:S(2)}, u32[]{:S(2)}) %collective-permute-start.17) | collective-permute-done | bytes 24608 | tf_op jit(solution)/shard_map/ppermute | solution.py:21
  (478 shorter events, 186.1 us)
Async XLA Ops:
  0.0 47.6 %collective-permute-start = (s32[1,2,512]{2,1,0:T(2,128)}, s32[1,2,512]{2,1,0:T(2,128)S(1)}, u32[]{:S(2)}, u32[]{:S(2)}) collective-permute-start(s32[1,2,512]{2,1,0:T(2,128)} %param.19), channel_id=1, source_target_pairs={{1,0},{2,1},{3,2},{4,3},{5,4},{6,5},{7,6},{8,7},{9,8},{10,9},{11,1... | collective-permute-start | bytes 12296 | tf_op jit(solution)/shard_map/ppermute | solution.py:21
  0.7 52.7 %collective-permute-start.2 = (s32[1,2,512]{2,1,0:T(2,128)}, s32[1,2,512]{2,1,0:T(2,128)S(1)}, u32[]{:S(2)}, u32[]{:S(2)}) collective-permute-start(s32[1,2,512]{2,1,0:T(2,128)} %param.19), channel_id=1, source_target_pairs={{0,1},{1,2},{2,3},{3,4},{4,5},{5,6},{6,7},{7,8},{8,9},{9,10},{10,1... | collective-permute-start | bytes 12296 | tf_op jit(solution)/shard_map/ppermute | solution.py:20
  6.1 47.9 %copy-start.17 = (s32[32,4096]{1,0:T(8,128)S(1)}, s32[32,4096]{1,0:T(8,128)}, u32[]{:S(2)}) copy-start(s32[32,4096]{1,0:T(8,128)} %param.18) | copy-start | bytes 1572868
  36.1 210.7 %collective-permute-start.8 = (bf16[1,3,4096]{2,1,0:T(4,128)(2,1)}, bf16[1,3,4096]{2,1,0:T(4,128)(2,1)}, u32[]{:S(2)}, u32[]{:S(2)}) collective-permute-start(bf16[1,3,4096]{2,1,0:T(4,128)(2,1)} %convert_bitcast_fusion.7), channel_id=1, source_target_pairs={{0,1},{1,2},{2,3},{3,4},{4,5},{5,6},{6,7},{7,8},{8,9},{9,10},{10,1... | collective-permute-start | bytes 73736 | tf_op jit(solution)/shard_map/ppermute | solution.py:20
  43.2 203.6 %collective-permute-start.9 = (bf16[1,3,4096]{2,1,0:T(4,128)(2,1)}, bf16[1,3,4096]{2,1,0:T(4,128)(2,1)}, u32[]{:S(2)}, u32[]{:S(2)}) collective-permute-start(bf16[1,3,4096]{2,1,0:T(4,128)(2,1)} %convert_bitcast_fusion.7), channel_id=1, source_target_pairs={{1,0},{2,1},{3,2},{4,3},{5,4},{6,5},{7,6},{8,7},{9,8},{10,9},{11,1... | collective-permute-start | bytes 73736 | tf_op jit(solution)/shard_map/ppermute | solution.py:21
  47.7 61.9 %copy-start.25 = (pred[32,512]{1,0:T(8,128)(4,1)}, pred[32,512]{1,0:T(8,128)(4,1)S(1)}, u32[]{:S(2)}) copy-start(pred[32,512]{1,0:T(8,128)(4,1)S(1)} %iota_compare_fusion.17) | copy-start | bytes 49156
  47.9 7.1 %collective-permute-start.1 = (bf16[3,512]{1,0:T(4,128)(2,1)S(1)}, bf16[3,512]{1,0:T(4,128)(2,1)S(1)}, u32[]{:S(2)}, u32[]{:S(2)}) collective-permute-start(bf16[3,512]{1,0:T(4,128)(2,1)S(1)} %select_convert_fusion.5), channel_id=1, source_target_pairs={{0,1},{1,2},{2,3},{3,4},{4,5},{5,6},{6,7},{7,8},{8,9},{9,10},{10,1... | collective-permute-start | bytes 9224 | tf_op jit(solution)/shard_map/ppermute | solution.py:29
  54.0 6.6 %collective-permute-start.3 = (bf16[3,512]{1,0:T(4,128)(2,1)S(1)}, bf16[3,512]{1,0:T(4,128)(2,1)S(1)}, u32[]{:S(2)}, u32[]{:S(2)}) collective-permute-start(bf16[3,512]{1,0:T(4,128)(2,1)S(1)} %select_convert_fusion.4), channel_id=1, source_target_pairs={{0,31},{1,0},{2,1},{3,2},{4,3},{5,4},{6,5},{7,6},{8,7},{9,8},{10,9... | collective-permute-start | bytes 9224 | tf_op jit(solution)/shard_map/ppermute | solution.py:29
  110.0 1.5 collective-permute-start.4
  110.2 6.9 %collective-permute-start.5 = (bf16[3,512]{1,0:T(4,128)(2,1)S(1)}, bf16[3,512]{1,0:T(4,128)(2,1)S(1)}, u32[]{:S(2)}, u32[]{:S(2)}) collective-permute-start(bf16[3,512]{1,0:T(4,128)(2,1)S(1)} %select_convert_fusion.2), channel_id=1, source_target_pairs={{0,31},{1,0},{2,1},{3,2},{4,3},{5,4},{6,5},{7,6},{8,7},{9,8},{10,9... | collective-permute-start | bytes 9224 | tf_op jit(solution)/shard_map/ppermute | solution.py:29
  179.1 1.3 collective-permute-start.6
  179.2 6.7 %collective-permute-start.7 = (bf16[3,512]{1,0:T(4,128)(2,1)S(1)}, bf16[3,512]{1,0:T(4,128)(2,1)S(1)}, u32[]{:S(2)}, u32[]{:S(2)}) collective-permute-start(bf16[3,512]{1,0:T(4,128)(2,1)S(1)} %select_convert_fusion), channel_id=1, source_target_pairs={{0,31},{1,0},{2,1},{3,2},{4,3},{5,4},{6,5},{7,6},{8,7},{9,8},{10,9... | collective-permute-start | bytes 9224 | tf_op jit(solution)/shard_map/ppermute | solution.py:29
  245.9 45.4 %copy-start.23 = (pred[32,4096]{1,0:T(8,128)(4,1)S(1)}, pred[32,4096]{1,0:T(8,128)(4,1)}, u32[]{:S(2)}) copy-start(pred[32,4096]{1,0:T(8,128)(4,1)} %iota_compare_fusion.13) | copy-start | bytes 393220
  245.9 45.4 %copy-start.30 = (s32[4096]{0:T(1024)S(1)}, s32[4096]{0:T(1024)}, u32[]{:S(2)}) copy-start(s32[4096]{0:T(1024)} %add_select_fusion.1) | copy-start | bytes 49156
  246.0 46.5 %copy-start.10 = (f32[3,4096]{1,0:T(4,128)S(1)}, f32[3,4096]{1,0:T(4,128)}, u32[]{:S(2)}) copy-start(f32[3,4096]{1,0:T(4,128)} %copy-done.8) | copy-start | bytes 147460
  246.0 46.5 %copy-start.12 = (f32[3,4096]{1,0:T(4,128)S(1)}, f32[3,4096]{1,0:T(4,128)}, u32[]{:S(2)}) copy-start(f32[3,4096]{1,0:T(4,128)} %copy-done.11) | copy-start | bytes 147460
  247.7 4.4 %collective-permute-start.10 = (bf16[1,3,4096]{2,1,0:T(4,128)(2,1)S(1)}, bf16[1,3,4096]{2,1,0:T(4,128)(2,1)S(1)}, u32[]{:S(2)}, u32[]{:S(2)}) collective-permute-start(bf16[1,3,4096]{2,1,0:T(4,128)(2,1)S(1)} %get-tuple-element.559), channel_id=1, source_target_pairs={{0,1},{1,2},{2,3},{3,4},{4,5},{5,6},{6,7},{7,8},{8,9},{9,10},{10,1... | collective-permute-start | bytes 73736 | tf_op jit(solution)/shard_map/ppermute | solution.py:20
  249.7 8.8 %collective-permute-start.11 = (bf16[1,3,4096]{2,1,0:T(4,128)(2,1)S(1)}, bf16[1,3,4096]{2,1,0:T(4,128)(2,1)S(1)}, u32[]{:S(2)}, u32[]{:S(2)}) collective-permute-start(bf16[1,3,4096]{2,1,0:T(4,128)(2,1)S(1)} %get-tuple-element.559), channel_id=1, source_target_pairs={{1,0},{2,1},{3,2},{4,3},{5,4},{6,5},{7,6},{8,7},{9,8},{10,9},{11,1... | collective-permute-start | bytes 73736 | tf_op jit(solution)/shard_map/ppermute | solution.py:21
  258.6 4.4 %collective-permute-start.12 = (bf16[1,3,4096]{2,1,0:T(4,128)(2,1)S(1)}, bf16[1,3,4096]{2,1,0:T(4,128)(2,1)S(1)}, u32[]{:S(2)}, u32[]{:S(2)}) collective-permute-start(bf16[1,3,4096]{2,1,0:T(4,128)(2,1)S(1)} %get-tuple-element.557), channel_id=1, source_target_pairs={{0,1},{1,2},{2,3},{3,4},{4,5},{5,6},{6,7},{7,8},{8,9},{9,10},{10,1... | collective-permute-start | bytes 73736 | tf_op jit(solution)/shard_map/ppermute | solution.py:20
  260.6 8.8 %collective-permute-start.13 = (bf16[1,3,4096]{2,1,0:T(4,128)(2,1)S(1)}, bf16[1,3,4096]{2,1,0:T(4,128)(2,1)S(1)}, u32[]{:S(2)}, u32[]{:S(2)}) collective-permute-start(bf16[1,3,4096]{2,1,0:T(4,128)(2,1)S(1)} %get-tuple-element.557), channel_id=1, source_target_pairs={{1,0},{2,1},{3,2},{4,3},{5,4},{6,5},{7,6},{8,7},{9,8},{10,9},{11,1... | collective-permute-start | bytes 73736 | tf_op jit(solution)/shard_map/ppermute | solution.py:21
  269.5 4.4 %collective-permute-start.14 = (bf16[1,3,4096]{2,1,0:T(4,128)(2,1)S(1)}, bf16[1,3,4096]{2,1,0:T(4,128)(2,1)S(1)}, u32[]{:S(2)}, u32[]{:S(2)}) collective-permute-start(bf16[1,3,4096]{2,1,0:T(4,128)(2,1)S(1)} %get-tuple-element.555), channel_id=1, source_target_pairs={{0,1},{1,2},{2,3},{3,4},{4,5},{5,6},{6,7},{7,8},{8,9},{9,10},{10,1... | collective-permute-start | bytes 73736 | tf_op jit(solution)/shard_map/ppermute | solution.py:20
  271.5 8.8 %collective-permute-start.15 = (bf16[1,3,4096]{2,1,0:T(4,128)(2,1)S(1)}, bf16[1,3,4096]{2,1,0:T(4,128)(2,1)S(1)}, u32[]{:S(2)}, u32[]{:S(2)}) collective-permute-start(bf16[1,3,4096]{2,1,0:T(4,128)(2,1)S(1)} %get-tuple-element.555), channel_id=1, source_target_pairs={{1,0},{2,1},{3,2},{4,3},{5,4},{6,5},{7,6},{8,7},{9,8},{10,9},{11,1... | collective-permute-start | bytes 73736 | tf_op jit(solution)/shard_map/ppermute | solution.py:21
  280.4 4.4 %collective-permute-start.16 = (bf16[1,3,4096]{2,1,0:T(4,128)(2,1)S(1)}, bf16[1,3,4096]{2,1,0:T(4,128)(2,1)S(1)}, u32[]{:S(2)}, u32[]{:S(2)}) collective-permute-start(bf16[1,3,4096]{2,1,0:T(4,128)(2,1)S(1)} %get-tuple-element.553), channel_id=1, source_target_pairs={{0,1},{1,2},{2,3},{3,4},{4,5},{5,6},{6,7},{7,8},{8,9},{9,10},{10,1... | collective-permute-start | bytes 73736 | tf_op jit(solution)/shard_map/ppermute | solution.py:20
  282.4 8.8 %collective-permute-start.17 = (bf16[1,3,4096]{2,1,0:T(4,128)(2,1)S(1)}, bf16[1,3,4096]{2,1,0:T(4,128)(2,1)S(1)}, u32[]{:S(2)}, u32[]{:S(2)}) collective-permute-start(bf16[1,3,4096]{2,1,0:T(4,128)(2,1)S(1)} %get-tuple-element.553), channel_id=1, source_target_pairs={{1,0},{2,1},{3,2},{4,3},{5,4},{6,5},{7,6},{8,7},{9,8},{10,9},{11,1... | collective-permute-start | bytes 73736 | tf_op jit(solution)/shard_map/ppermute | solution.py:21
  (37 other events, 149.7 us)
